TPU v7x, 128 devices: a whole 4x4x4 slice. The times are simulated.
128 devices in a mesh: row: 8 (over z, x_lo), col: 16 (over y, x_hi, core).
Axes of the slice: x: 4 (x_hi: 2, x_lo: 2; x = x_hi * 2 + x_lo), y: 4, z: 4, core: 2. Of those that a mesh axis runs over, the one named last changes fastest.
Arguments:
- tensor_blocks: bfloat16 [8, 384, 6, 128, 128], P('row', 'col'), may hold values from -6 to 6
- block_list: int32 [8, 384, 2], P('row', 'col'), may hold values from 0 to 15, as said below
- occ_green: bfloat16 [2048, 2048], P(('row', 'col')), may hold values from -0.125 to 0.125
- virt_green: bfloat16 [2048, 2048], P(None, ('row', 'col')), may hold values from -0.125 to 0.125
Outputs:
- polarizability: float32 [8, 6, 6], P('row')
Inputs may be any that keep to these rules, and one draw needn't show every extreme that they name: `block_list`: within the 24 blocks of one device the (m, l) pairs are distinct, every atom block occurs as l once or twice and as m once or twice, so at most 2 blocks of one device share an l, and some l is shared by exactly 2.
All inputs are finite; a program needn't handle non-finite values.
Results may differ from a plain program's by a relative error of at most 0.006.
Values may be sent and summed in bfloat16 or wider, within the bound.
No kernel may reach another device: no remote copies, remote signals or barrier semaphores. Data moves between devices by JAX's collectives and lax.ppermute only.
A program may use at most 128 MiB of HBM per device.

v0:
```python
import jax
import jax.numpy as jnp
from jax import lax
from jax.sharding import PartitionSpec as P

CAP = 2


def shards(tensor_blocks, block_list, occ_green, virt_green):
    col_count = lax.axis_size("col")
    blocks = tensor_blocks[0]
    pairs = block_list[0]
    held = blocks.shape[0]
    width = blocks.shape[-1]
    target = pairs[:, 1]
    first_blocks = pairs[:, 0]
    places = jnp.arange(held)
    slot_rank = jnp.sum(
        (target[None, :] == target[:, None]) & (places[None, :] < places[:, None]), axis=1
    )
    select = (target[:, None, None] == jnp.arange(col_count)[None, :, None]) & (
        slot_rank[:, None, None] == jnp.arange(CAP)[None, None, :]
    )
    send_blocks = jnp.einsum(
        "tdk,tpab->dkpab", select.astype(jnp.bfloat16), blocks, preferred_element_type=jnp.float32
    ).astype(jnp.bfloat16)
    send_first = jnp.sum(select.astype(jnp.int32) * (first_blocks + 1)[:, None, None], axis=0) - 1
    recv_blocks, recv_first = (
        lax.all_to_all(send_blocks, "col", split_axis=0, concat_axis=0, tiled=True),
        lax.all_to_all(send_first, "col", split_axis=0, concat_axis=0, tiled=True),
    )
    slot_total = recv_blocks.shape[0] * recv_blocks.shape[1]
    flat_blocks = recv_blocks.reshape(slot_total, recv_blocks.shape[2], width, width)
    placing = (recv_first.reshape(slot_total)[:, None] == jnp.arange(col_count)[None, :]).astype(
        jnp.bfloat16
    )
    dense_parts = jnp.einsum(
        "sm,spab->pmab", placing, flat_blocks, preferred_element_type=jnp.float32
    )
    dense_tensor = dense_parts.astype(jnp.bfloat16).reshape(
        flat_blocks.shape[1], col_count * width, width
    )
    basis_total = dense_tensor.shape[1]
    occ_half = jnp.einsum(
        "nm,pml->pnl",
        lax.all_gather(occ_green, ("row", "col"), axis=0, tiled=True),
        dense_tensor,
        preferred_element_type=jnp.float32,
    ).astype(jnp.bfloat16)
    turned = lax.all_to_all(occ_half, "col", split_axis=1, concat_axis=2, tiled=True)
    both_sides = jnp.einsum(
        "pnl,ls->pns",
        turned,
        lax.all_gather(virt_green, ("row", "col"), axis=1, tiled=True),
        preferred_element_type=jnp.float32,
    ).astype(jnp.bfloat16)
    partial_polar = jnp.einsum(
        "pns,qsn->pq", both_sides, dense_tensor, preferred_element_type=jnp.float32
    )
    polar_total = lax.psum(partial_polar, "col")
    return (polar_total / float(basis_total))[None]


def solution(mesh):
    in_specs = (
        P("row", "col", None, None, None),
        P("row", "col", None),
        P(("row", "col"), None),
        P(None, ("row", "col")),
    )
    out_specs = P("row", None, None)
    return jax.shard_map(shards, mesh=mesh, in_specs=in_specs, out_specs=out_specs, check_vma=False)
```

profile of v0, /device:TPU:0, one launch (start us, length us, event | category | flops | bytes accessed | tf_op | source)
XLA Modules:
  0.0 585.8 jit_solution(11802510145233425043)
XLA Ops:
  6.5 0.7 all-gather.3.cloned.1.call-update
  7.3 0.7 all-gather.5.cloned.1.call-update
  8.0 0.8 add_bitcast_fusion.1
  9.1 0.7 copy.44
  9.8 7.1 %all-to-all-start.1 = ((s32[16,1,2]{2,1,0:T(1,128)}), s32[16,1,2]{2,1,0:T(1,128)S(1)}, u32[]{:S(2)}, u32[]{:S(2)}) async-start(s32[16,1,2]{2,1,0:T(1,128)} %copy.44), calls=%async_computation.1 | async-start | bytes 16384 | tf_op jit(solution)/shard_map/all_to_all | solution.py:30
  16.9 6.1 %fusion.11 = bf16[16,2,6,128,128]{4,0,3,2,1:T(8,128)(2,1)S(1)} fusion(bf16[24,6,128,128]{3,2,1,0:T(8,128)(2,1)} %bitcast.54, pred[24,2]{0,1:T(4,128)(4,1)S(1)} %iota_compare_fusion.3, pred[24,16]{0,1:T(8,128)(4,1)S(1)} %iota_compare_fusion.2), kind=kOutput, calls=%fused_computation.11 | convolution fusion | flops 154141440 | bytes 11010480 | tf_op jit(solution)/shard_map/tdk,tpab->dkpab/dot_general | solution.py:24
  23.0 4.3 copy.43
  27.4 7.3 %all-to-all-start = ((bf16[16,2,6,128,128]{4,3,2,1,0:T(8,128)(2,1)}), bf16[16,2,6,128,128]{4,3,2,1,0:T(8,128)(2,1)}, u32[]{:S(2)}, u32[]{:S(2)}) async-start(bf16[16,2,6,128,128]{4,3,2,1,0:T(8,128)(2,1)} %copy.43), calls=%async_computation | async-start | bytes 12582912 | tf_op jit(solution)/shard_map/all_to_all | solution.py:29
  35.2 0.7 reduce.3
  35.9 78.0 %all-to-all-done = bf16[16,2,6,128,128]{4,3,2,1,0:T(8,128)(2,1)} async-done(((bf16[16,2,6,128,128]{4,3,2,1,0:T(8,128)(2,1)}), bf16[16,2,6,128,128]{4,3,2,1,0:T(8,128)(2,1)}, u32[]{:S(2)}, u32[]{:S(2)}) %all-to-all-start) | async-done | bytes 6291488 | tf_op jit(solution)/shard_map/all_to_all | solution.py:29
  113.9 6.6 %convert_bitcast_fusion = bf16[6,16,128,128]{3,1,2,0:T(8,128)(2,1)S(1)} fusion(bf16[32,6,128,128]{3,2,1,0:T(8,128)(2,1)} %bitcast.6, s32[32]{0:T(128)S(1)} %eq.73), kind=kOutput, calls=%fused_computation.14 | convolution fusion | flops 102236672 | bytes 9437312 | tf_op jit(solution)/shard_map/sm,spab->pmab/dot_general | solution.py:37
  120.5 0.8 copy.46
  121.3 159.5 %all-gather.3.cloned.1.call-done = bf16[2048,2048]{1,0:T(8,128)(2,1)} async-done(((bf16[16,2048]{1,0:T(8,128)(2,1)}), bf16[2048,2048]{1,0:T(8,128)(2,1)}) %all-gather.3.cloned.1.call-update) | async-done | bytes 8388624 | tf_op jit(solution)/shard_map/all_gather | solution.py:46
  280.8 10.3 %fusion.20 = bf16[6,2048,128]{1,2,0:T(8,128)(2,1)} fusion(bf16[6,2048,128]{2,1,0:T(8,128)(2,1)S(1)} %bitcast.52, bf16[2048,2048]{1,0:T(8,128)(2,1)} %all-gather.3.cloned.1.call-done), kind=kOutput, calls=%fused_computation.15 | convolution fusion | flops 6444023808 | bytes 14680064 | tf_op jit(solution)/shard_map/nm,pml->pnl/dot_general | solution.py:44
  291.2 6.4 %copy.48 = bf16[6,2048,128]{2,0,1:T(8,128)(2,1)} copy(bf16[6,2048,128]{1,2,0:T(8,128)(2,1)} %fusion.20) | data formatting | bytes 6291456 | tf_op jit(solution)/shard_map/convert_element_type | solution.py:49
  297.6 5.4 all-to-all-start.2
  303.0 5.1 copy.53
  308.0 51.2 %all-to-all-done.2 = bf16[6,2048,128]{2,0,1:T(8,128)(2,1)} async-done(((bf16[6,2048,128]{2,0,1:T(8,128)(2,1)}), bf16[6,2048,128]{2,0,1:T(8,128)(2,1)}, u32[]{:S(2)}, u32[]{:S(2)}) %all-to-all-start.2) | async-done | bytes 3145760 | tf_op jit(solution)/shard_map/all_to_all | solution.py:50
  359.3 5.4 copy.50
  364.7 164.0 %all-gather.5.cloned.1.call-done = bf16[2048,2048]{0,1:T(8,128)(2,1)} async-done(((bf16[2048,16]{0,1:T(8,128)(2,1)}), bf16[2048,2048]{0,1:T(8,128)(2,1)}) %all-gather.5.cloned.1.call-update) | async-done | bytes 8388624 | tf_op jit(solution)/shard_map/all_gather | solution.py:54
  528.7 9.3 %fusion.17 = bf16[6,128,2048]{2,1,0:T(8,128)(2,1)S(1)} fusion(bf16[6,128,2048]{1,2,0:T(8,128)(2,1)S(1)} %bitcast.55, bf16[2048,2048]{0,1:T(8,128)(2,1)} %all-gather.5.cloned.1.call-done), kind=kOutput, calls=%fused_computation.13 | convolution fusion | flops 6444023808 | bytes 14680064 | tf_op jit(solution)/shard_map/pnl,ls->pns/dot_general | solution.py:51
  538.0 5.7 fusion.25
  543.7 34.6 %psum.7 = f32[6,6]{1,0:T(8,128)S(1)} all-reduce(f32[6,6]{1,0:T(8,128)S(1)} %fusion.25), channel_id=1, replica_groups=mesh['row'=8,'col'=16] {'col'}, use_global_device_ids=true, to_apply=%region_2.0 | all-reduce | flops 36 | bytes 288 | tf_op jit(solution)/shard_map/psum | solution.py:60
  578.4 0.6 copy.54
  (13 shorter events, 1.0 us)
Async XLA Ops:
  6.5 274.3 %all-gather.3.cloned.1.call-start = ((), (), s32[]{:S(2)}) async-start(), calls=%async_computation.3 | async-start | bytes 8454144 | tf_op jit(solution)/shard_map/all_gather | solution.py:46
  7.3 521.5 %all-gather.5.cloned.1.call-start = ((), (), s32[]{:S(2)}) async-start(), calls=%async_computation.4 | async-start | bytes 8454144 | tf_op jit(solution)/shard_map/all_gather | solution.py:54
  9.8 17.6 %all-to-all-start.1 = ((s32[16,1,2]{2,1,0:T(1,128)}), s32[16,1,2]{2,1,0:T(1,128)S(1)}, u32[]{:S(2)}, u32[]{:S(2)}) async-start(s32[16,1,2]{2,1,0:T(1,128)} %copy.44), calls=%async_computation.1 | async-start | bytes 16384 | tf_op jit(solution)/shard_map/all_to_all | solution.py:30
  27.4 86.5 %all-to-all-start = ((bf16[16,2,6,128,128]{4,3,2,1,0:T(8,128)(2,1)}), bf16[16,2,6,128,128]{4,3,2,1,0:T(8,128)(2,1)}, u32[]{:S(2)}, u32[]{:S(2)}) async-start(bf16[16,2,6,128,128]{4,3,2,1,0:T(8,128)(2,1)} %copy.43), calls=%async_computation | async-start | bytes 12582912 | tf_op jit(solution)/shard_map/all_to_all | solution.py:29
  297.6 61.7 %all-to-all-start.2 = ((bf16[6,2048,128]{2,0,1:T(8,128)(2,1)}), bf16[6,2048,128]{2,0,1:T(8,128)(2,1)}, u32[]{:S(2)}, u32[]{:S(2)}) async-start(bf16[6,2048,128]{2,0,1:T(8,128)(2,1)} %copy.48), calls=%async_computation.2 | async-start | bytes 8388608 | tf_op jit(solution)/shard_map/all_to_all | solution.py:50
  528.7 9.3 %copy-start = (bf16[6,2048,128]{1,0,2:T(8,128)(2,1)S(1)}, bf16[6,2048,128]{1,0,2:T(8,128)(2,1)}, u32[]{:S(2)}) copy-start(bf16[6,2048,128]{1,0,2:T(8,128)(2,1)} %copy.53) | copy-start | bytes 9437188
Sparse Core Ops, SparseCore 0:
  9.1 271.7 all-gather.2
  282.6 246.1 all-gather.4
where the time goes:
time: 586 us
  waiting for transfers between devices  454 us (77%)
  matrix products  38 us (6%)
  blocking collectives  34.6 us (6%)
  local copies, waits for them, and re-layouts  23.9 us (4%)
  starting transfers between devices  19.8 us (3%)
  between operations  13.5 us (2%)
    all_gather x1, waiting for transfers between devices, shards(): lax.all_gather(virt_green, ('row', 'col'), axis=1, tiled=True)  164 us
    all_gather x1, waiting for transfers between devices, shards(): lax.all_gather(occ_green, ('row', 'col'), axis=0, tiled=True)  160 us
    all_to_all x1, waiting for transfers between devices, shards(): lax.all_to_all(send_blocks, 'col', split_axis=0, concat_axis=0, tiled=True)  78 us
    all_to_all x1, waiting for transfers between devices, shards(): lax.all_to_all(occ_half, 'col', split_axis=1, concat_axis=2, tiled=True)  51.2 us
    psum x1, blocking collectives, shards(): polar_total = lax.psum(partial_polar, 'col')  34.6 us
  transfers between devices with their start and end apart: 5, of which 4 were waited for; matrix products, arithmetic and copies ran while one was open for 8% of the time, Pallas kernels for 0%

commit v1 on v0

--- a/solution.py
+++ b/solution.py
@@ -57,7 +57,8 @@
     partial_polar = jnp.einsum(
         "pns,qsn->pq", both_sides, dense_tensor, preferred_element_type=jnp.float32
     )
-    polar_total = lax.psum(partial_polar, "col")
+    parts = lax.all_gather(partial_polar, "col", axis=0, tiled=False)
+    polar_total = parts.sum(axis=0)
     return (polar_total / float(basis_total))[None]
 
 

time: 586 us -> 575 us (0.981)
  blocking collectives: 34.6 us -> 21.7 us
    psum x1 -> x0, blocking collectives: 34.6 us -> none  [shards(): polar_total = lax.psum(partial_polar, 'col')]
    all_gather x0 -> x1, blocking collectives: none -> 21.7 us  [shards(): parts = lax.all_gather(partial_polar, 'col', axis=0, tiled=False)]
where the time goes in v1:
time: 575 us; the launch traced here: 573 us
  waiting for transfers between devices  454 us (79%)
  matrix products  38 us (7%)
  local copies, waits for them, and re-layouts  23.9 us (4%)
  blocking collectives  21.7 us (4%)
  starting transfers between devices  19.8 us (3%)
  between operations  13.5 us (2%)
    all_gather x1, waiting for transfers between devices, shards(): lax.all_gather(virt_green, ('row', 'col'), axis=1, tiled=True)  164 us
    all_gather x1, waiting for transfers between devices, shards(): lax.all_gather(occ_green, ('row', 'col'), axis=0, tiled=True)  160 us
    all_to_all x1, waiting for transfers between devices, shards(): lax.all_to_all(send_blocks, 'col', split_axis=0, concat_axis=0, tiled=True)  78 us
    all_to_all x1, waiting for transfers between devices, shards(): lax.all_to_all(occ_half, 'col', split_axis=1, concat_axis=2, tiled=True)  51.2 us
    all_gather x1, blocking collectives, shards(): parts = lax.all_gather(partial_polar, 'col', axis=0, tiled=False)  21.7 us
  transfers between devices with their start and end apart: 5, of which 4 were waited for; matrix products, arithmetic and copies ran while one was open for 8% of the time, Pallas kernels for 0%

profile of v1, /device:TPU:0, one launch (start us, length us, event | category | flops | bytes accessed | tf_op | source)
XLA Modules:
  0.0 572.8 jit_solution(8799092122873661746)
XLA Ops:
  6.5 0.7 all-gather.5.cloned.1.call-update
  7.3 0.7 all-gather.7.cloned.1.call-update
  8.0 0.8 add_bitcast_fusion.1
  9.1 0.7 copy.44
  9.8 7.1 %all-to-all-start.1 = ((s32[16,1,2]{2,1,0:T(1,128)}), s32[16,1,2]{2,1,0:T(1,128)S(1)}, u32[]{:S(2)}, u32[]{:S(2)}) async-start(s32[16,1,2]{2,1,0:T(1,128)} %copy.44), calls=%async_computation.1 | async-start | bytes 16384 | tf_op jit(solution)/shard_map/all_to_all | solution.py:30
  16.9 6.1 %fusion.11 = bf16[16,2,6,128,128]{4,0,3,2,1:T(8,128)(2,1)S(1)} fusion(bf16[24,6,128,128]{3,2,1,0:T(8,128)(2,1)} %bitcast.55, pred[24,2]{0,1:T(4,128)(4,1)S(1)} %iota_compare_fusion.3, pred[24,16]{0,1:T(8,128)(4,1)S(1)} %iota_compare_fusion.2), kind=kOutput, calls=%fused_computation.11 | convolution fusion | flops 154141440 | bytes 11010480 | tf_op jit(solution)/shard_map/tdk,tpab->dkpab/dot_general | solution.py:24
  23.0 4.3 copy.43
  27.4 7.3 %all-to-all-start = ((bf16[16,2,6,128,128]{4,3,2,1,0:T(8,128)(2,1)}), bf16[16,2,6,128,128]{4,3,2,1,0:T(8,128)(2,1)}, u32[]{:S(2)}, u32[]{:S(2)}) async-start(bf16[16,2,6,128,128]{4,3,2,1,0:T(8,128)(2,1)} %copy.43), calls=%async_computation | async-start | bytes 12582912 | tf_op jit(solution)/shard_map/all_to_all | solution.py:29
  35.2 0.7 reduce.4
  35.9 78.0 %all-to-all-done = bf16[16,2,6,128,128]{4,3,2,1,0:T(8,128)(2,1)} async-done(((bf16[16,2,6,128,128]{4,3,2,1,0:T(8,128)(2,1)}), bf16[16,2,6,128,128]{4,3,2,1,0:T(8,128)(2,1)}, u32[]{:S(2)}, u32[]{:S(2)}) %all-to-all-start) | async-done | bytes 6291488 | tf_op jit(solution)/shard_map/all_to_all | solution.py:29
  113.9 6.6 %convert_bitcast_fusion = bf16[6,16,128,128]{3,1,2,0:T(8,128)(2,1)S(1)} fusion(bf16[32,6,128,128]{3,2,1,0:T(8,128)(2,1)} %bitcast.6, s32[32]{0:T(128)S(1)} %eq.73), kind=kOutput, calls=%fused_computation.14 | convolution fusion | flops 102236672 | bytes 9437312 | tf_op jit(solution)/shard_map/sm,spab->pmab/dot_general | solution.py:37
  120.5 0.8 copy.46
  121.3 159.5 %all-gather.5.cloned.1.call-done = bf16[2048,2048]{1,0:T(8,128)(2,1)} async-done(((bf16[16,2048]{1,0:T(8,128)(2,1)}), bf16[2048,2048]{1,0:T(8,128)(2,1)}) %all-gather.5.cloned.1.call-update) | async-done | bytes 8388624 | tf_op jit(solution)/shard_map/all_gather | solution.py:46
  280.8 10.3 %fusion.20 = bf16[6,2048,128]{1,2,0:T(8,128)(2,1)} fusion(bf16[6,2048,128]{2,1,0:T(8,128)(2,1)S(1)} %bitcast.53, bf16[2048,2048]{1,0:T(8,128)(2,1)} %all-gather.5.cloned.1.call-done), kind=kOutput, calls=%fused_computation.15 | convolution fusion | flops 6444023808 | bytes 14680064 | tf_op jit(solution)/shard_map/nm,pml->pnl/dot_general | solution.py:44
  291.2 6.4 %copy.48 = bf16[6,2048,128]{2,0,1:T(8,128)(2,1)} copy(bf16[6,2048,128]{1,2,0:T(8,128)(2,1)} %fusion.20) | data formatting | bytes 6291456 | tf_op jit(solution)/shard_map/convert_element_type | solution.py:49
  297.6 5.4 all-to-all-start.2
  303.0 5.1 copy.53
  308.0 51.2 %all-to-all-done.2 = bf16[6,2048,128]{2,0,1:T(8,128)(2,1)} async-done(((bf16[6,2048,128]{2,0,1:T(8,128)(2,1)}), bf16[6,2048,128]{2,0,1:T(8,128)(2,1)}, u32[]{:S(2)}, u32[]{:S(2)}) %all-to-all-start.2) | async-done | bytes 3145760 | tf_op jit(solution)/shard_map/all_to_all | solution.py:50
  359.3 5.4 copy.50
  364.7 164.0 %all-gather.7.cloned.1.call-done = bf16[2048,2048]{0,1:T(8,128)(2,1)} async-done(((bf16[2048,16]{0,1:T(8,128)(2,1)}), bf16[2048,2048]{0,1:T(8,128)(2,1)}) %all-gather.7.cloned.1.call-update) | async-done | bytes 8388624 | tf_op jit(solution)/shard_map/all_gather | solution.py:54
  528.7 9.3 %fusion.17 = bf16[6,128,2048]{2,1,0:T(8,128)(2,1)S(1)} fusion(bf16[6,128,2048]{1,2,0:T(8,128)(2,1)S(1)} %bitcast.56, bf16[2048,2048]{0,1:T(8,128)(2,1)} %all-gather.7.cloned.1.call-done), kind=kOutput, calls=%fused_computation.13 | convolution fusion | flops 6444023808 | bytes 14680064 | tf_op jit(solution)/shard_map/pnl,ls->pns/dot_general | solution.py:51
  538.0 5.7 fusion.25
  543.7 21.7 %all-gather.1 = f32[16,6,6]{2,1,0:T(8,128)S(1)} all-gather(f32[1,6,6]{2,1,0:T(8,128)S(1)} %fusion.25), channel_id=2, replica_groups=mesh['row'=8,'col'=16] {'col'}, dimensions={0}, use_global_device_ids=true | all-gather | bytes 2448 | tf_op jit(solution)/shard_map/all_gather | solution.py:60
  565.4 0.6 copy.54
  (14 shorter events, 1.0 us)
Async XLA Ops:
  6.5 274.3 %all-gather.5.cloned.1.call-start = ((), (), s32[]{:S(2)}) async-start(), calls=%async_computation.3 | async-start | bytes 8454144 | tf_op jit(solution)/shard_map/all_gather | solution.py:46
  7.3 521.5 %all-gather.7.cloned.1.call-start = ((), (), s32[]{:S(2)}) async-start(), calls=%async_computation.4 | async-start | bytes 8454144 | tf_op jit(solution)/shard_map/all_gather | solution.py:54
  9.8 17.6 %all-to-all-start.1 = ((s32[16,1,2]{2,1,0:T(1,128)}), s32[16,1,2]{2,1,0:T(1,128)S(1)}, u32[]{:S(2)}, u32[]{:S(2)}) async-start(s32[16,1,2]{2,1,0:T(1,128)} %copy.44), calls=%async_computation.1 | async-start | bytes 16384 | tf_op jit(solution)/shard_map/all_to_all | solution.py:30
  27.4 86.5 %all-to-all-start = ((bf16[16,2,6,128,128]{4,3,2,1,0:T(8,128)(2,1)}), bf16[16,2,6,128,128]{4,3,2,1,0:T(8,128)(2,1)}, u32[]{:S(2)}, u32[]{:S(2)}) async-start(bf16[16,2,6,128,128]{4,3,2,1,0:T(8,128)(2,1)} %copy.43), calls=%async_computation | async-start | bytes 12582912 | tf_op jit(solution)/shard_map/all_to_all | solution.py:29
  297.6 61.7 %all-to-all-start.2 = ((bf16[6,2048,128]{2,0,1:T(8,128)(2,1)}), bf16[6,2048,128]{2,0,1:T(8,128)(2,1)}, u32[]{:S(2)}, u32[]{:S(2)}) async-start(bf16[6,2048,128]{2,0,1:T(8,128)(2,1)} %copy.48), calls=%async_computation.2 | async-start | bytes 8388608 | tf_op jit(solution)/shard_map/all_to_all | solution.py:50
  528.7 9.3 %copy-start = (bf16[6,2048,128]{1,0,2:T(8,128)(2,1)S(1)}, bf16[6,2048,128]{1,0,2:T(8,128)(2,1)}, u32[]{:S(2)}) copy-start(bf16[6,2048,128]{1,0,2:T(8,128)(2,1)} %copy.53) | copy-start | bytes 9437188
Sparse Core Ops, SparseCore 0:
  9.1 271.7 all-gather.4
  282.6 246.1 all-gather.6
